TPU v7x, 512 devices: a whole 4x4x16 slice. The times are simulated.
512 devices in a mesh: dst: 32 (over z, core), src: 16 (over y, x).
Axes of the slice: x: 4, y: 4, z: 16, core: 2. Of those that a mesh axis runs over, the one named last changes fastest.
Arguments:
- adj_tiles: bfloat16 [32, 16, 64, 64, 512], P('dst', 'src'), may hold values from 0 to 0.011047363
- tile_cols: int32 [32, 16, 64, 8], P('dst', 'src'), may hold values from 0 to 63
- send_block: int32 [32, 16, 32, 2], P('dst', 'src'), may hold values from 0 to 15
- send_count: int32 [32, 16, 32], P('dst', 'src'), may hold values from 1 to 2, as said below
- history: bfloat16 [64, 16, 8192], P('dst', 'src'), may hold values from -6 to 6
- node_feats: bfloat16 [512, 8192], P('dst', 'src'), may hold values from -6 to 6
- w_neigh: bfloat16 [128, 128], replicated, may hold values from -0.5 to 0.5
- w_self: bfloat16 [128, 128], replicated, may hold values from -0.5 to 0.5
- out_bias: float32 [128], replicated, may hold values from -3 to 3
- cotangent: bfloat16 [512, 8192], P('dst', 'src'), may hold values from -6 to 6
Outputs:
- new_embed: bfloat16 [512, 8192], P('dst', 'src')
- grad_neigh: float32 [128, 128], replicated
- grad_self: float32 [128, 128], replicated
- grad_bias: float32 [128], replicated
Inputs may be any that keep to these rules, and one draw needn't show every extreme that they name: `send_count`: in every draw, for each source group some owner gets 2 live slots from every device of that group.
All inputs are finite; a program needn't handle non-finite values.
Results may differ from a plain program's by a relative error of at most 0.0052.
Values may be sent and summed in bfloat16 or wider, within the bound.
A program may use at most 64 MiB of HBM per device.

v0:
```python
import jax
import jax.numpy as jnp
from jax import lax
from jax.sharding import PartitionSpec as P


def on_device(
    adj_tiles,
    tile_cols,
    send_block,
    send_count,
    history,
    node_feats,
    w_neigh,
    w_self,
    out_bias,
    cotangent,
):
    owners = lax.axis_size("dst")
    groups = lax.axis_size("src")
    slot_count = adj_tiles.shape[2]
    block_size = adj_tiles.shape[3]
    feat_width = w_neigh.shape[0]
    capacity = slot_count // owners
    own_blocks = node_feats.shape[0]
    gathered = lax.all_gather(history, "dst", axis=0, tiled=True)
    group_table = gathered.reshape(-1, block_size, feat_width)
    picked = group_table[tile_cols.reshape(-1)].reshape(slot_count, -1, feat_width)
    tiles_flat = adj_tiles.reshape(slot_count, block_size, -1)
    partial_value = jnp.einsum(
        "sir,srf->sif", tiles_flat, picked, preferred_element_type=jnp.float32
    )
    alive_mask = (jnp.arange(capacity)[None, :] < send_count.reshape(owners, 1)).astype(jnp.float32)
    partial_value = (
        partial_value.reshape(owners, capacity, block_size * feat_width) * alive_mask[:, :, None]
    )
    targets = send_block.reshape(owners, capacity)
    spread = jnp.broadcast_to(targets[:, :, None], (owners, capacity, groups))
    arrived, arrived_ids = (
        lax.all_to_all(
            lax.all_to_all(partial_value, "dst", split_axis=0, concat_axis=0, tiled=True),
            "src",
            split_axis=2,
            concat_axis=1,
            tiled=True,
        ),
        lax.all_to_all(
            lax.all_to_all(spread, "dst", split_axis=0, concat_axis=0, tiled=True),
            "src",
            split_axis=2,
            concat_axis=1,
            tiled=True,
        ),
    )
    selector = (arrived_ids.reshape(1, -1) == jnp.arange(own_blocks)[:, None]).astype(jnp.float32)
    summed = jnp.dot(
        selector,
        arrived.reshape(selector.shape[1], -1),
        precision=lax.Precision.HIGHEST,
        preferred_element_type=jnp.float32,
    )
    agg_rows = summed.astype(jnp.bfloat16).reshape(-1, feat_width)
    self_rows = node_feats.reshape(-1, feat_width)
    pre_act = (
        jnp.dot(agg_rows, w_neigh, preferred_element_type=jnp.float32)
        + jnp.dot(self_rows, w_self, preferred_element_type=jnp.float32)
        + out_bias
    )
    sigmoid_z = jax.nn.sigmoid(pre_act)
    new_embed = (pre_act * sigmoid_z).astype(jnp.bfloat16).reshape(node_feats.shape)
    loss_scale = float(own_blocks * owners * block_size) ** (-0.5)
    slope = sigmoid_z * (1.0 + pre_act * (1.0 - sigmoid_z))
    grad_pre = cotangent.reshape(-1, feat_width).astype(jnp.float32) * slope * loss_scale
    grad_low = grad_pre.astype(jnp.bfloat16)
    grad_neigh = jnp.dot(agg_rows.T, grad_low, preferred_element_type=jnp.float32)
    grad_self = jnp.dot(self_rows.T, grad_low, preferred_element_type=jnp.float32)
    grad_bias = jnp.sum(grad_pre, axis=0)
    grad_neigh, grad_self, grad_bias = lax.psum((grad_neigh, grad_self, grad_bias), ("dst", "src"))
    return (new_embed, grad_neigh, grad_self, grad_bias)


def solution(mesh):
    in_specs = (
        P("dst", "src", None, None, None),
        P("dst", "src", None, None),
        P("dst", "src", None, None),
        P("dst", "src", None),
        P("dst", "src", None),
        P("dst", "src"),
        P(),
        P(),
        P(),
        P("dst", "src"),
    )
    out_specs = (P("dst", "src"), P(), P(), P())
    return jax.shard_map(
        on_device, mesh=mesh, in_specs=in_specs, out_specs=out_specs, check_vma=False
    )
```

profile of v0, /device:TPU:1, one launch (start us, length us, event | category | flops | bytes accessed | tf_op | source)
XLA Modules:
  0.0 780.6 jit_solution(10505770939572856301)
XLA Ops:
  7.2 1.4 copy.38
  8.7 0.8 copy.35
  9.5 0.7 broadcast_in_dim.5
  10.2 16.8 %all-to-all-start = ((s32[32,2,16]{2,1,0:T(2,128)}), s32[32,2,16]{2,1,0:T(2,128)S(1)}, u32[]{:S(2)}, u32[]{:S(2)}) async-start(s32[32,2,16]{2,1,0:T(2,128)} %broadcast_in_dim.5), calls=%async_computation | async-start | bytes 65536 | tf_op jit(solution)/shard_map/all_to_all | solution.py:48
  26.9 0.8 copy.39
  27.8 0.7 fusion.7
  28.5 59.7 %all-gather.2.cloned.1.call-done = bf16[64,1,8192]{2,1,0:T(2,128)(2,1)} async-done(((bf16[2,1,8192]{2,1,0:T(2,128)(2,1)}), bf16[64,1,8192]{2,1,0:T(2,128)(2,1)}) %all-gather.2.cloned.1.call-update) | async-done | bytes 1048592 | tf_op jit(solution)/shard_map/all_gather | solution.py:26
  88.3 7.9 %reduce = bf16[64,8192]{1,0:T(8,128)(2,1)S(1)} reduce(bf16[64,1,8192]{2,1,0:T(2,128)(2,1)} %all-gather.2.cloned.1.call-done, bf16[]{:T(256)} %constant.17), dimensions={1}, to_apply=%all_gather.3.reduce_sub_computation | reduce | bytes 2097154 | tf_op jit(solution)/shard_map/all_gather | solution.py:26
  96.4 13.5 %gather_fusion = bf16[512,64,128]{2,1,0:T(8,128)(2,1)} fusion(bf16[64,64,128]{2,1,0:T(8,128)(2,1)S(1)} %bitcast.38, s32[1024]{0:T(1024)S(1)} %pad_clamp_fusion), kind=kCustom, calls=%fused_computation | custom fusion | bytes 16779264 | tf_op jit(solution)/shard_map/gather | solution.py:28
  109.9 6.3 fusion.2
  116.3 2.2 reshape.102
  118.5 4.2 broadcast_multiply_fusion
  122.7 8.2 %all-to-all-start.2 = ((f32[32,2,8192]{2,1,0:T(2,128)}), f32[32,2,8192]{2,1,0:T(2,128)S(1)}, u32[]{:S(2)}, u32[]{:S(2)}) async-start(f32[32,2,8192]{2,1,0:T(2,128)} %broadcast_multiply_fusion), calls=%async_computation.2 | async-start | bytes 4194304 | tf_op jit(solution)/shard_map/all_to_all | solution.py:41
  131.0 0.7 copy.36
  131.6 97.9 %all-to-all-done.2 = f32[32,2,8192]{2,1,0:T(2,128)S(1)} async-done(((f32[32,2,8192]{2,1,0:T(2,128)}), f32[32,2,8192]{2,1,0:T(2,128)S(1)}, u32[]{:S(2)}, u32[]{:S(2)}) %all-to-all-start.2) | async-done | bytes 2097184 | tf_op jit(solution)/shard_map/all_to_all | solution.py:41
  229.6 6.4 all-to-all-start.1
  236.0 8.6 %copy.40 = f32[32,2,8192]{0,1,2:T(2,128)} copy(f32[32,2,8192]{2,1,0:T(2,128)S(1)} %all-to-all-done.2) | data formatting | bytes 4194304 | tf_op jit(solution)/shard_map/all_to_all | solution.py:41
  244.6 11.4 %reshape.117 = f32[16,1,32768]{2,1,0:T(1,128)} reshape(f32[8192,2,32]{2,1,0:T(2,128)} %bitcast.40) | data formatting | bytes 4194304
  256.0 6.8 all-to-all-start.3
  263.3 27.6 %all-to-all-done.3 = f32[16,1,32768]{2,1,0:T(1,128)S(1)} async-done(((f32[16,1,32768]{2,1,0:T(1,128)}), f32[16,1,32768]{2,1,0:T(1,128)S(1)}, u32[]{:S(2)}, u32[]{:S(2)}) %all-to-all-start.3) | async-done | bytes 2097184 | tf_op jit(solution)/shard_map/all_to_all | solution.py:40
  290.9 1.3 copy-done.1
  292.8 7.3 reduce.1
  300.1 9.2 %reshape.118 = f32[8192,2,32]{2,1,0:T(2,128)} reshape(f32[16,32768]{1,0:T(8,128)S(1)} %reduce.1) | data formatting | bytes 4194304
  309.3 10.3 %copy.41 = f32[32,2,16,512]{3,1,2,0:T(2,128)S(1)} copy(f32[32,2,16,512]{0,1,3,2:T(2,128)} %bitcast.41) | data formatting | bytes 4194304 | tf_op jit(solution)/shard_map/all_to_all | solution.py:40
  319.6 2.5 reshape.103
  322.1 2.4 convolution_convert_fusion
  324.9 0.8 convolution_bitcast_fusion
  325.7 0.8 fusion.9
  327.2 103.9 %psum.23 = f32[128]{0:T(128)} all-reduce(f32[128]{0:T(128)S(1)} %get-tuple-element.26), channel_id=1, replica_groups=mesh['dst'=32,'src'=16] {'dst','src'}, use_global_device_ids=true, to_apply=%region_3.0 | all-reduce | flops 128 | bytes 1024 | tf_op jit(solution)/shard_map/psum | solution.py:78
  431.1 339.6 %all-reduce.3.cloned.1.call-done = (f32[128,128]{1,0:T(8,128)}, f32[128,128]{0,1:T(8,128)}) async-done(((f32[128,128]{1,0:T(8,128)}, f32[128,128]{0,1:T(8,128)}), (f32[128,128]{1,0:T(8,128)}, f32[128,128]{0,1:T(8,128)})) %all-reduce.3.cloned.1.call-update) | async-done | bytes 131088 | tf_op jit(solution)/shard_map/psum | solution.py:78
  770.7 1.6 copy.42
  772.3 1.5 copy.46
  (30 shorter events, 2.4 us)
Async XLA Ops:
  7.2 317.5 %copy-start = (bf16[128,128]{1,0:T(8,128)(2,1)S(1)}, bf16[128,128]{1,0:T(8,128)(2,1)}, u32[]{:S(2)}) copy-start(bf16[128,128]{1,0:T(8,128)(2,1)} %param.17) | copy-start | bytes 98308
  7.2 81.1 %all-gather.2.cloned.1.call-start = ((), (), s32[]{:S(2)}) async-start(), calls=%async_computation.4 | async-start | bytes 2162688 | tf_op jit(solution)/shard_map/all_gather | solution.py:26
  10.2 112.5 %all-to-all-start = ((s32[32,2,16]{2,1,0:T(2,128)}), s32[32,2,16]{2,1,0:T(2,128)S(1)}, u32[]{:S(2)}, u32[]{:S(2)}) async-start(s32[32,2,16]{2,1,0:T(2,128)} %broadcast_in_dim.5), calls=%async_computation | async-start | bytes 65536 | tf_op jit(solution)/shard_map/all_to_all | solution.py:48
  122.7 106.9 %all-to-all-start.2 = ((f32[32,2,8192]{2,1,0:T(2,128)}), f32[32,2,8192]{2,1,0:T(2,128)S(1)}, u32[]{:S(2)}, u32[]{:S(2)}) async-start(f32[32,2,8192]{2,1,0:T(2,128)} %broadcast_multiply_fusion), calls=%async_computation.2 | async-start | bytes 4194304 | tf_op jit(solution)/shard_map/all_to_all | solution.py:41
  229.6 26.4 %all-to-all-start.1 = ((s32[32,2,16]{0,1,2:T(2,128)}), s32[32,2,16]{0,1,2:T(2,128)S(1)}, u32[]{:S(2)}, u32[]{:S(2)}) async-start(s32[32,2,16]{0,1,2:T(2,128)} %copy.36), calls=%async_computation.1 | async-start | bytes 32768 | tf_op jit(solution)/shard_map/all_to_all | solution.py:47
  256.0 6.9 copy-start.4
  256.0 6.9 copy-start.3
  256.0 34.9 %all-to-all-start.3 = ((f32[16,1,32768]{2,1,0:T(1,128)}), f32[16,1,32768]{2,1,0:T(1,128)S(1)}, u32[]{:S(2)}, u32[]{:S(2)}) async-start(f32[16,1,32768]{2,1,0:T(1,128)} %reshape.117), calls=%async_computation.3 | async-start | bytes 4194304 | tf_op jit(solution)/shard_map/all_to_all | solution.py:40
  262.8 507.9 %all-reduce.3.cloned.1.call-start = ((), (), s32[]{:S(2)}) async-start(), calls=%async_computation.5 | async-start | bytes 262144 | tf_op jit(solution)/shard_map/psum | solution.py:78
  290.9 1.3 copy-start.1
  322.1 2.4 copy-start.2
  322.1 2.6 copy-start.5
Sparse Core Ops, SparseCore 0:
  10.7 77.5 all-gather.1
  326.7 444.0 all-reduce.2
where the time goes:
time: 782 us; the launch traced here: 781 us
  waiting for transfers between devices  525 us (67%)
  blocking collectives  104 us (13%)
  local copies, waits for them, and re-layouts  68.5 us (9%)
  starting transfers between devices  38.3 us (5%)
  other arithmetic  20.1 us (3%)
  between operations  14.2 us (2%)
  matrix products  10.6 us (1%)
    psum x1, waiting for transfers between devices, on_device(): lax.psum((grad_neigh, grad_self, grad_bias), ('dst', 'src'))  340 us
    psum x1, blocking collectives, on_device(): lax.psum((grad_neigh, grad_self, grad_bias), ('dst', 'src'))  104 us
    all_to_all x1, waiting for transfers between devices, on_device(): lax.all_to_all(partial_value, 'dst', split_axis=0, concat_axis=0, tiled=T...  97.9 us
    all_gather x1, waiting for transfers between devices, on_device(): gathered = lax.all_gather(history, 'dst', axis=0, tiled=True)  59.7 us
    all_to_all x1, waiting for transfers between devices, on_device(): lax.all_to_all(lax.all_to_all(partial_value, 'dst', split_axis=0, concat_...  27.6 us
    unnamed x19, local copies, waits for them, and re-layouts  27.5 us
    all_to_all x1, starting transfers between devices, on_device(): lax.all_to_all(spread, 'dst', split_axis=0, concat_axis=0, tiled=True)  16.8 us
  transfers between devices with their start and end apart: 6, of which 4 were waited for; matrix products, arithmetic and copies ran while one was open for 8% of the time, Pallas kernels for 0%

commit v1 on v0

--- a/solution.py
+++ b/solution.py
@@ -16,6 +16,11 @@
     out_bias,
     cotangent,
 ):
+
+    def review_marks(message):
+        r_now = lax.psum(lax.psum(message, axis_name="dst"), "src")
+        return r_now
+
     owners = lax.axis_size("dst")
     groups = lax.axis_size("src")
     slot_count = adj_tiles.shape[2]
@@ -75,7 +80,7 @@
     grad_neigh = jnp.dot(agg_rows.T, grad_low, preferred_element_type=jnp.float32)
     grad_self = jnp.dot(self_rows.T, grad_low, preferred_element_type=jnp.float32)
     grad_bias = jnp.sum(grad_pre, axis=0)
-    grad_neigh, grad_self, grad_bias = lax.psum((grad_neigh, grad_self, grad_bias), ("dst", "src"))
+    grad_neigh, grad_self, grad_bias = review_marks((grad_neigh, grad_self, grad_bias))
     return (new_embed, grad_neigh, grad_self, grad_bias)
 
 

time: 782 us -> 640 us (0.82)
  waiting for transfers between devices: 525 us -> 407 us
  blocking collectives: 104 us -> 80.2 us
    psum x1 -> x2, waiting for transfers between devices: 340 us -> 221 us  [review_marks(): r_now = lax.psum(lax.psum(message, axis_name='dst'), 'src')]
    psum x1 -> x2, blocking collectives: 104 us -> 80.2 us  [review_marks(): r_now = lax.psum(lax.psum(message, axis_name='dst'), 'src')]
  transfers between devices with their start and end apart: 6 -> 7, of which waited for: 4 -> 5; matrix products, arithmetic and copies ran while one was open for 8% -> 9% of each run, Pallas kernels for 0% -> 0%
where the time goes in v1:
time: 640 us; the launch traced here: 638 us
  waiting for transfers between devices  407 us (64%)
  blocking collectives  80.2 us (13%)
  local copies, waits for them, and re-layouts  68.4 us (11%)
  starting transfers between devices  38.4 us (6%)
  other arithmetic  20.1 us (3%)
  between operations  13.9 us (2%)
  matrix products  10.6 us (2%)
    psum x2, waiting for transfers between devices, review_marks(): r_now = lax.psum(lax.psum(message, axis_name='dst'), 'src')  221 us
    all_to_all x1, waiting for transfers between devices, on_device(): lax.all_to_all(partial_value, 'dst', split_axis=0, concat_axis=0, tiled=T...  97.9 us
    psum x2, blocking collectives, review_marks(): r_now = lax.psum(lax.psum(message, axis_name='dst'), 'src')  80.2 us
    all_gather x1, waiting for transfers between devices, on_device(): gathered = lax.all_gather(history, 'dst', axis=0, tiled=True)  59.7 us
    all_to_all x1, waiting for transfers between devices, on_device(): lax.all_to_all(lax.all_to_all(partial_value, 'dst', split_axis=0, concat_...  27.6 us
    unnamed x19, local copies, waits for them, and re-layouts  27.5 us
    all_to_all x1, starting transfers between devices, on_device(): lax.all_to_all(spread, 'dst', split_axis=0, concat_axis=0, tiled=True)  16.8 us
    gather x1, local copies, waits for them, and re-layouts, on_device(): group_table[tile_cols.reshape(-1)].reshape(slot_count, -1, feat_width)  13.5 us
  transfers between devices with their start and end apart: 7, of which 5 were waited for; matrix products, arithmetic and copies ran while one was open for 9% of the time, Pallas kernels for 0%

profile of v1, /device:TPU:1, one launch (start us, length us, event | category | flops | bytes accessed | tf_op | source)
XLA Modules:
  0.0 638.3 jit_solution(12921014070610407846)
XLA Ops:
  7.2 1.4 copy.38
  8.7 0.8 copy.35
  10.2 16.8 %all-to-all-start = ((s32[32,2,16]{2,1,0:T(2,128)}), s32[32,2,16]{2,1,0:T(2,128)S(1)}, u32[]{:S(2)}, u32[]{:S(2)}) async-start(s32[32,2,16]{2,1,0:T(2,128)} %broadcast_in_dim.5), calls=%async_computation | async-start | bytes 65536 | tf_op jit(solution)/shard_map/all_to_all | solution.py:53
  26.9 0.8 copy.39
  27.8 0.7 fusion.7
  28.5 59.7 %all-gather.2.cloned.1.call-done = bf16[64,1,8192]{2,1,0:T(2,128)(2,1)} async-done(((bf16[2,1,8192]{2,1,0:T(2,128)(2,1)}), bf16[64,1,8192]{2,1,0:T(2,128)(2,1)}) %all-gather.2.cloned.1.call-update) | async-done | bytes 1048592 | tf_op jit(solution)/shard_map/all_gather | solution.py:31
  88.3 7.9 %reduce = bf16[64,8192]{1,0:T(8,128)(2,1)S(1)} reduce(bf16[64,1,8192]{2,1,0:T(2,128)(2,1)} %all-gather.2.cloned.1.call-done, bf16[]{:T(256)} %constant.17), dimensions={1}, to_apply=%all_gather.3.reduce_sub_computation | reduce | bytes 2097154 | tf_op jit(solution)/shard_map/all_gather | solution.py:31
  96.4 13.5 %gather_fusion = bf16[512,64,128]{2,1,0:T(8,128)(2,1)} fusion(bf16[64,64,128]{2,1,0:T(8,128)(2,1)S(1)} %bitcast.38, s32[1024]{0:T(1024)S(1)} %pad_clamp_fusion), kind=kCustom, calls=%fused_computation | custom fusion | bytes 16779264 | tf_op jit(solution)/shard_map/gather | solution.py:33
  109.9 6.3 fusion.2
  116.3 2.2 reshape.102
  118.5 4.2 broadcast_multiply_fusion
  122.7 8.2 %all-to-all-start.2 = ((f32[32,2,8192]{2,1,0:T(2,128)}), f32[32,2,8192]{2,1,0:T(2,128)S(1)}, u32[]{:S(2)}, u32[]{:S(2)}) async-start(f32[32,2,8192]{2,1,0:T(2,128)} %broadcast_multiply_fusion), calls=%async_computation.2 | async-start | bytes 4194304 | tf_op jit(solution)/shard_map/all_to_all | solution.py:46
  131.7 97.9 %all-to-all-done.2 = f32[32,2,8192]{2,1,0:T(2,128)S(1)} async-done(((f32[32,2,8192]{2,1,0:T(2,128)}), f32[32,2,8192]{2,1,0:T(2,128)S(1)}, u32[]{:S(2)}, u32[]{:S(2)}) %all-to-all-start.2) | async-done | bytes 2097184 | tf_op jit(solution)/shard_map/all_to_all | solution.py:46
  229.6 6.4 %all-to-all-start.1 = ((s32[32,2,16]{0,1,2:T(2,128)}), s32[32,2,16]{0,1,2:T(2,128)S(1)}, u32[]{:S(2)}, u32[]{:S(2)}) async-start(s32[32,2,16]{0,1,2:T(2,128)} %copy.36), calls=%async_computation.1 | async-start | bytes 32768 | tf_op jit(solution)/shard_map/all_to_all | solution.py:52
  236.0 8.5 %copy.40 = f32[32,2,8192]{0,1,2:T(2,128)} copy(f32[32,2,8192]{2,1,0:T(2,128)S(1)} %all-to-all-done.2) | data formatting | bytes 4194304 | tf_op jit(solution)/shard_map/all_to_all | solution.py:46
  244.5 11.4 %reshape.117 = f32[16,1,32768]{2,1,0:T(1,128)} reshape(f32[8192,2,32]{2,1,0:T(2,128)} %bitcast.40) | data formatting | bytes 4194304
  255.9 6.8 %all-to-all-start.3 = ((f32[16,1,32768]{2,1,0:T(1,128)}), f32[16,1,32768]{2,1,0:T(1,128)S(1)}, u32[]{:S(2)}, u32[]{:S(2)}) async-start(f32[16,1,32768]{2,1,0:T(1,128)} %reshape.117), calls=%async_computation.3 | async-start | bytes 4194304 | tf_op jit(solution)/shard_map/all_to_all | solution.py:45
  263.2 27.6 %all-to-all-done.3 = f32[16,1,32768]{2,1,0:T(1,128)S(1)} async-done(((f32[16,1,32768]{2,1,0:T(1,128)}), f32[16,1,32768]{2,1,0:T(1,128)S(1)}, u32[]{:S(2)}, u32[]{:S(2)}) %all-to-all-start.3) | async-done | bytes 2097184 | tf_op jit(solution)/shard_map/all_to_all | solution.py:45
  290.8 1.3 copy-done.1
  292.7 7.3 %reduce.1 = f32[16,32768]{1,0:T(8,128)S(1)} reduce(f32[16,1,32768]{2,1,0:T(1,128)} %copy-done.1, f32[]{:T(128)} %broadcast.40), dimensions={1}, to_apply=%all_to_all.33.reduce_sub_computation | reduce | bytes 4194308 | tf_op jit(solution)/shard_map/all_to_all | solution.py:45
  300.0 9.2 %reshape.118 = f32[8192,2,32]{2,1,0:T(2,128)} reshape(f32[16,32768]{1,0:T(8,128)S(1)} %reduce.1) | data formatting | bytes 4194304
  309.2 10.3 %copy.41 = f32[32,2,16,512]{3,1,2,0:T(2,128)S(1)} copy(f32[32,2,16,512]{0,1,3,2:T(2,128)} %bitcast.41) | data formatting | bytes 4194304 | tf_op jit(solution)/shard_map/all_to_all | solution.py:45
  319.6 2.5 reshape.103
  322.1 2.4 convolution_convert_fusion
  324.8 0.8 convolution_bitcast_fusion
  325.6 0.8 fusion.9
  326.5 191.0 %all-reduce.5.cloned.1.call-done = (f32[128,128]{1,0:T(8,128)}, f32[128,128]{0,1:T(8,128)}) async-done(((f32[128,128]{1,0:T(8,128)}, f32[128,128]{0,1:T(8,128)}), (f32[128,128]{1,0:T(8,128)}, f32[128,128]{0,1:T(8,128)})) %all-reduce.5.cloned.1.call-update) | async-done | bytes 131088 | tf_op jit(solution)/shard_map/psum | solution.py:21
  518.2 46.1 %psum.46 = f32[128]{0:T(128)S(1)} all-reduce(f32[128]{0:T(128)S(1)} %get-tuple-element.28), channel_id=1, replica_groups=mesh['dst'=32,'src'=16] {'dst'}, use_global_device_ids=true, to_apply=%region_5.0 | all-reduce | flops 128 | bytes 1024 | tf_op jit(solution)/shard_map/psum | solution.py:21
  564.2 34.1 %psum.47 = f32[128]{0:T(128)} all-reduce(f32[128]{0:T(128)S(1)} %psum.46), channel_id=1, replica_groups=mesh['dst'=32,'src'=16] {'src'}, use_global_device_ids=true, to_apply=%region_6.0 | all-reduce | flops 128 | bytes 1024 | tf_op jit(solution)/shard_map/psum | solution.py:21
  598.4 30.4 %all-reduce.7.cloned.1.call-done = (f32[128,128]{1,0:T(8,128)}, f32[128,128]{0,1:T(8,128)}) async-done(((f32[128,128]{1,0:T(8,128)}, f32[128,128]{0,1:T(8,128)}), (f32[128,128]{1,0:T(8,128)}, f32[128,128]{0,1:T(8,128)})) %all-reduce.7.cloned.1.call-update) | async-done | bytes 131088 | tf_op jit(solution)/shard_map/psum | solution.py:21
  628.7 1.6 copy.42
  630.3 1.5 copy.48
  (34 shorter events, 3.9 us)
Async XLA Ops:
  7.2 317.5 %copy-start = (bf16[128,128]{1,0:T(8,128)(2,1)S(1)}, bf16[128,128]{1,0:T(8,128)(2,1)}, u32[]{:S(2)}) copy-start(bf16[128,128]{1,0:T(8,128)(2,1)} %param.17) | copy-start | bytes 98308
  7.2 81.1 %all-gather.2.cloned.1.call-start = ((), (), s32[]{:S(2)}) async-start(), calls=%async_computation.4 | async-start | bytes 2162688 | tf_op jit(solution)/shard_map/all_gather | solution.py:31
  10.2 112.6 %all-to-all-start = ((s32[32,2,16]{2,1,0:T(2,128)}), s32[32,2,16]{2,1,0:T(2,128)S(1)}, u32[]{:S(2)}, u32[]{:S(2)}) async-start(s32[32,2,16]{2,1,0:T(2,128)} %broadcast_in_dim.5), calls=%async_computation | async-start | bytes 65536 | tf_op jit(solution)/shard_map/all_to_all | solution.py:53
  122.7 106.9 %all-to-all-start.2 = ((f32[32,2,8192]{2,1,0:T(2,128)}), f32[32,2,8192]{2,1,0:T(2,128)S(1)}, u32[]{:S(2)}, u32[]{:S(2)}) async-start(f32[32,2,8192]{2,1,0:T(2,128)} %broadcast_multiply_fusion), calls=%async_computation.2 | async-start | bytes 4194304 | tf_op jit(solution)/shard_map/all_to_all | solution.py:46
  229.6 26.3 %all-to-all-start.1 = ((s32[32,2,16]{0,1,2:T(2,128)}), s32[32,2,16]{0,1,2:T(2,128)S(1)}, u32[]{:S(2)}, u32[]{:S(2)}) async-start(s32[32,2,16]{0,1,2:T(2,128)} %copy.36), calls=%async_computation.1 | async-start | bytes 32768 | tf_op jit(solution)/shard_map/all_to_all | solution.py:52
  255.9 6.9 %copy-start.4 = (bf16[16,512]{1,0:T(8,128)(2,1)S(1)}, bf16[16,512]{1,0:T(8,128)(2,1)}, u32[]{:S(2)}) copy-start(bf16[16,512]{1,0:T(8,128)(2,1)} %param.15) | copy-start | bytes 49156
  255.9 6.9 %copy-start.3 = (bf16[16,512]{1,0:T(8,128)(2,1)S(1)}, bf16[16,512]{1,0:T(8,128)(2,1)}, u32[]{:S(2)}) copy-start(bf16[16,512]{1,0:T(8,128)(2,1)} %param.19) | copy-start | bytes 49156
  255.9 34.9 %all-to-all-start.3 = ((f32[16,1,32768]{2,1,0:T(1,128)}), f32[16,1,32768]{2,1,0:T(1,128)S(1)}, u32[]{:S(2)}, u32[]{:S(2)}) async-start(f32[16,1,32768]{2,1,0:T(1,128)} %reshape.117), calls=%async_computation.3 | async-start | bytes 4194304 | tf_op jit(solution)/shard_map/all_to_all | solution.py:45
  262.7 254.8 %all-reduce.5.cloned.1.call-start = ((), (), s32[]{:S(2)}) async-start(), calls=%async_computation.5 | async-start | bytes 262144 | tf_op jit(solution)/shard_map/psum | solution.py:21
  290.8 1.3 copy-start.1
  322.1 2.4 copy-start.2
  322.1 2.6 copy-start.5
  326.5 302.3 %all-reduce.7.cloned.1.call-start = ((), (), s32[]{:S(2)}) async-start(), calls=%async_computation.6 | async-start | bytes 262144 | tf_op jit(solution)/shard_map/psum | solution.py:21
Sparse Core Ops, SparseCore 0:
  10.7 77.5 all-gather.1
  326.6 190.8 all-reduce.4
  521.1 107.5 all-reduce.6
